TPU v7x, 128 devices: a whole 4x4x4 slice. The times are simulated.
128 devices in a mesh: section: 2 (over z_hi), seq: 8 (over x, z_lo), expert: 8 (over y, core).
Axes of the slice: x: 4, y: 4, z: 4 (z_hi: 2, z_lo: 2; z = z_hi * 2 + z_lo), core: 2. Of those that a mesh axis runs over, the one named last changes fastest.
Arguments:
- tokens: bfloat16 [2, 1024, 2048], P(None, ('seq', 'expert')), may hold values from -12 to 12
- prompt_lengths: int32 [2, 3], replicated, may hold values from 1 to 512, 1024 in all within a row
- cache_lengths: int32 [2, 3], replicated, may hold values from 1 to 1024, 2048 in all within a row
- kv_cache: bfloat16 [2, 2048, 2, 2048], P(None, 'seq', None, 'expert'), may hold values from -360 to 360
- attn_routes: int32 [2, 1024, 2], P(None, 'seq'), may hold values from 0 to 3, all different within a row
- ffn_routes: int32 [2, 1024, 2], P(None, ('seq', 'expert')), may hold values from 0 to 7, all different within a row; in each aligned block of 16 rows (0 to 15, 16 to 31, ..., all dimensions but the last counted through in order) at most 8 rows name the same one
- attn_gain: float32 [2048], replicated, may hold values from 0.1 to 1.9
- ffn_gain: float32 [2048], replicated, may hold values from 0.1 to 1.9
- attn_mix: bfloat16 [2048, 4], replicated, may hold values from -0.125 to 0.125
- query_weight: bfloat16 [2048, 4, 2048], P(None, None, 'expert'), may hold values from -0.125 to 0.125
- kv_weight: bfloat16 [2048, 2, 2048], P(None, None, 'expert'), may hold values from -0.125 to 0.125
- out_weight: bfloat16 [4, 2048, 2048], P(None, 'expert'), may hold values from -0.125 to 0.125
- ffn_mix: bfloat16 [2048, 8], replicated, may hold values from -0.125 to 0.125
- in_weight: bfloat16 [8, 2048, 2, 5632], P('expert', None, None, 'seq'), may hold values from -0.125 to 0.125
- down_weight: bfloat16 [8, 5632, 2048], P('expert', 'seq'), may hold values from -0.078125 to 0.078125
Outputs:
- layer_out: bfloat16 [2, 1024, 2048], P('section', ('seq', 'expert'))
Inputs may be any that keep to these rules, and one draw needn't show every extreme that they name: `prompt_lengths`: each row sums to 1024; its largest entry is 512. `cache_lengths`: each row sums to 2048; its largest entry is 1024. `attn_routes`: the two experts of a position differ; every expert is named somewhere. `ffn_routes`: the two experts of a position differ. Taking all micro-batches and positions in order, in each aligned block of 16 positions (the rows of one device) no expert is named more than 8 times, and some block names one exactly 8 times.
All inputs are finite; a program needn't handle non-finite values.
Results may differ from a plain program's by a relative error of at most 0.029.
Values may be sent and summed in bfloat16 or wider, within the bound.
A program may use at most 128 MiB of HBM per device.

v0:
```python
import jax
import jax.numpy as jnp
from jax import lax
from jax.sharding import PartitionSpec as P

HEAD_DIM = 128
EPS = 1e-06
THETA = 10000.0
NEGATIVE = -1e30


def passed_along(value, axis, steps):
    count = lax.axis_size(axis)
    initial, last = (max(0, -steps), min(count, count - steps))
    return lax.ppermute(value, axis, [(source, source + steps) for source in range(initial, last)])


def rms_scale(values, gain):
    widened = values.astype(jnp.float32)
    inverse = lax.rsqrt(jnp.mean(widened * widened, axis=-1, keepdims=True) + EPS)
    return (widened * inverse * gain).astype(jnp.bfloat16)


def segment_of(row_index, lengths):
    ends = jnp.cumsum(lengths)
    return jnp.sum((row_index[:, None] >= ends[None, :]).astype(jnp.int32), axis=1)


def positions(row_index, lengths, cached):
    ends = jnp.cumsum(lengths)
    segment = jnp.sum((row_index[:, None] >= ends[None, :]).astype(jnp.int32), axis=1)
    matched = segment[:, None] == jnp.arange(lengths.shape[0], dtype=jnp.int32)[None, :]
    begins = jnp.sum(jnp.where(matched, (ends - lengths)[None, :], 0), axis=1)
    offsets = jnp.sum(jnp.where(matched, cached[None, :], 0), axis=1)
    return (segment, offsets + row_index - begins)


def rotate(values, place):
    half_dim = values.shape[-1] // 2
    freq = THETA ** (-jnp.arange(half_dim, dtype=jnp.float32) / half_dim)
    angle = place.astype(jnp.float32)[:, None] * freq[None, :]
    shape = (values.shape[0],) + (1,) * (values.ndim - 2) + (half_dim,)
    cosine = jnp.cos(angle).reshape(shape)
    sine = jnp.sin(angle).reshape(shape)
    former = values[..., :half_dim]
    latter = values[..., half_dim:]
    return jnp.concatenate(
        [former * cosine - latter * sine, latter * cosine + former * sine], axis=-1
    )


def route_gates(normed, mixing, routes):
    logits = jnp.dot(normed, mixing, preferred_element_type=jnp.float32)
    chosen = jnp.take_along_axis(logits, routes, axis=1)
    leading = jax.nn.sigmoid(chosen[:, 0] - chosen[:, 1])
    return jnp.stack([leading, 1.0 - leading], axis=1)


def select_batch(values, batch):
    return lax.dynamic_index_in_dim(values, batch, 0, keepdims=False)


def attention_block(
    own_rows, lengths, cached, cache_rows, routes, gain, mixing, query_weight, kv_weight, out_weight
):
    gathered = lax.all_gather(own_rows, "expert", axis=0, tiled=True)
    count = gathered.shape[0]
    normed = rms_scale(gathered, gain)
    row_index = lax.axis_index("seq") * count + jnp.arange(count, dtype=jnp.int32)
    segment, place = positions(row_index, lengths, cached)
    gates = route_gates(normed, mixing, routes)
    experts = query_weight.shape[1]
    width = query_weight.shape[2]
    local_heads = width // HEAD_DIM
    query_all = jnp.dot(
        normed, query_weight.reshape(query_weight.shape[0], -1), preferred_element_type=jnp.float32
    )
    query_all = query_all.reshape(count, experts, local_heads, HEAD_DIM)
    query = jnp.take_along_axis(query_all, routes[:, :, None, None], axis=1)
    query = rotate(query, place).astype(jnp.bfloat16)
    queries = query.reshape(count * 2, local_heads, HEAD_DIM)
    projected = jnp.dot(
        normed, kv_weight.reshape(kv_weight.shape[0], -1), preferred_element_type=jnp.float32
    )
    projected = projected.reshape(count, 2, local_heads, HEAD_DIM)
    fresh_keys = rotate(projected[:, 0], place).astype(jnp.bfloat16).reshape(count, width)
    fresh_values = projected[:, 1].astype(jnp.bfloat16).reshape(count, width)
    fresh = jnp.stack([fresh_keys, fresh_values], axis=1)
    query_segment = jnp.repeat(segment, 2)
    query_index = jnp.repeat(row_index, 2)
    scale = HEAD_DIM ** (-0.5)
    slots = count * 2

    def absorb(carried, piece, allowed):
        row_top, row_total, row_sum = carried
        keys = piece[:, 0].reshape(-1, local_heads, HEAD_DIM)
        values = piece[:, 1].reshape(-1, local_heads, HEAD_DIM)
        scores = (
            jnp.einsum("qhd,khd->hqk", queries, keys, preferred_element_type=jnp.float32) * scale
        )
        scores = jnp.where(allowed[None], scores, NEGATIVE)
        new_top = jnp.maximum(row_top, jnp.max(scores, axis=2))
        weights = jnp.where(allowed[None], jnp.exp(scores - new_top[:, :, None]), 0.0)
        shrink = jnp.exp(row_top - new_top)
        row_total = row_total * shrink + jnp.sum(weights, axis=2)
        row_sum = row_sum * shrink[:, :, None] + jnp.einsum(
            "hqk,khd->hqd", weights.astype(jnp.bfloat16), values, preferred_element_type=jnp.float32
        )
        return (new_top, row_total, row_sum)

    initial = (
        jnp.full((local_heads, slots), NEGATIVE, jnp.float32),
        jnp.zeros((local_heads, slots), jnp.float32),
        jnp.zeros((local_heads, slots, HEAD_DIM), jnp.float32),
    )
    piece = lax.all_gather(cache_rows, "seq", axis=0, tiled=True)
    key_segment = segment_of(jnp.arange(piece.shape[0], dtype=jnp.int32), cached)
    allowed = query_segment[:, None] == key_segment[None, :]
    carried = absorb(initial, piece, allowed)
    piece = lax.all_gather(fresh, "seq", axis=0, tiled=True)
    key_index = jnp.arange(piece.shape[0], dtype=jnp.int32)
    key_segment = segment_of(key_index, lengths)
    allowed = (query_segment[:, None] == key_segment[None, :]) & (
        key_index[None, :] <= query_index[:, None]
    )
    row_top, row_total, row_sum = absorb(carried, piece, allowed)
    attended = (row_sum / row_total[:, :, None]).astype(jnp.bfloat16)
    attended = attended.transpose(1, 0, 2).reshape(count, 2, width)
    select = (routes[:, :, None] == jnp.arange(experts, dtype=jnp.int32)[None, None, :]).astype(
        jnp.float32
    )
    select = select * gates[:, :, None]
    spread = jnp.einsum("tka,tkd->tad", select, attended.astype(jnp.float32)).astype(jnp.bfloat16)
    spread = spread.reshape(count, experts * width)
    out_flat = out_weight.reshape(experts * width, -1)
    term = lax.psum_scatter(
        jnp.dot(spread, out_flat, preferred_element_type=jnp.float32).astype(jnp.bfloat16),
        "expert",
        scatter_dimension=0,
        tiled=True,
    ).astype(jnp.float32)
    return (own_rows.astype(jnp.float32) + term).astype(jnp.bfloat16)


def expert_hidden(rows, in_weight):
    single = in_weight[0]
    both = jnp.dot(rows, single.reshape(single.shape[0], -1), preferred_element_type=jnp.float32)
    both = both.reshape(rows.shape[0], 2, -1)
    return (jax.nn.silu(both[:, 0]) * both[:, 1]).astype(jnp.bfloat16)


def expert_block(middle, routes, gain, mixing, in_weight, down_weight):
    rows = middle.shape[0]
    features = middle.shape[1]
    normed = rms_scale(middle, gain)
    gates = route_gates(normed, mixing, routes)
    experts = mixing.shape[1]
    capacity = max(2, 4 * rows // experts)
    flat = routes.reshape(-1)
    member = (flat[:, None] == jnp.arange(experts, dtype=jnp.int32)[None, :]).astype(jnp.int32)
    earlier = jnp.cumsum(member, axis=0) - member
    slot = jnp.sum(earlier * member, axis=1)
    target = flat * capacity + slot
    table = (jnp.arange(experts * capacity, dtype=jnp.int32)[:, None] == target[None, :]).astype(
        jnp.bfloat16
    )
    table = jnp.sum(table.reshape(experts * capacity, rows, 2), axis=2)
    buffer = jnp.dot(table, normed, preferred_element_type=jnp.float32).astype(jnp.bfloat16)
    buffer = buffer.reshape(experts, capacity, features)
    seq_count = lax.axis_size("seq")
    copies = jnp.broadcast_to(buffer[None], (seq_count,) + buffer.shape)
    copies = copies.reshape(seq_count * experts, capacity, features)
    arrived = lax.all_to_all(copies, ("seq", "expert"), split_axis=0, concat_axis=0, tiled=True)
    flat_rows = arrived.reshape(-1, features)
    hidden = expert_hidden(flat_rows, in_weight)
    partial_value = jnp.dot(hidden, down_weight[0], preferred_element_type=jnp.float32)
    partial_value = partial_value.astype(jnp.bfloat16).reshape(arrived.shape)
    returned = lax.all_to_all(
        partial_value, ("seq", "expert"), split_axis=0, concat_axis=0, tiled=True
    )
    results = jnp.sum(
        returned.reshape(seq_count, experts, capacity, features).astype(jnp.float32), axis=0
    )
    picked = jnp.take(results.reshape(experts * capacity, features), target, axis=0).reshape(
        rows, 2, features
    )
    mixture = gates[:, 0:1] * picked[:, 0] + gates[:, 1:2] * picked[:, 1]
    return (middle.astype(jnp.float32) + mixture).astype(jnp.bfloat16)


def on_device(
    tokens,
    prompt_lengths,
    cache_lengths,
    kv_cache,
    attn_routes,
    ffn_routes,
    attn_gain,
    ffn_gain,
    attn_mix,
    query_weight,
    kv_weight,
    out_weight,
    ffn_mix,
    in_weight,
    down_weight,
):
    batches = tokens.shape[0]
    half_count = batches // 2
    section = lax.axis_index("section")

    def attend(batch):
        return attention_block(
            select_batch(tokens, batch),
            select_batch(prompt_lengths, batch),
            select_batch(cache_lengths, batch),
            select_batch(kv_cache, batch),
            select_batch(attn_routes, batch),
            attn_gain,
            attn_mix,
            query_weight,
            kv_weight,
            out_weight,
        )

    def finish(middle, batch):
        return expert_block(
            middle, select_batch(ffn_routes, batch), ffn_gain, ffn_mix, in_weight, down_weight
        )

    blank = jnp.zeros(tokens.shape[1:], jnp.bfloat16)
    first_section = section == 0

    def one_tick(incoming, tick):
        ahead = jnp.minimum(tick, batches - 1)
        behind = jnp.maximum(tick - 1, 0)
        attended_rows = attend(ahead)
        finished_rows = finish(incoming, behind)
        produced = jnp.where(first_section, attended_rows, finished_rows)
        passed = passed_along(produced, "section", 1)
        return (passed, produced)

    ticks = jnp.arange(batches + 1, dtype=jnp.int32)
    _, produced_all = lax.scan(one_tick, blank, ticks)
    finished = produced_all[1:]
    former_half = finished[:half_count]
    latter_half = finished[half_count:]
    returned = passed_along(former_half, "section", -1)
    return jnp.where(first_section, returned, latter_half)


def solution(mesh):
    return jax.shard_map(
        on_device,
        mesh=mesh,
        in_specs=(
            P(None, ("seq", "expert"), None),
            P(),
            P(),
            P(None, "seq", None, "expert"),
            P(None, "seq", None),
            P(None, ("seq", "expert"), None),
            P(),
            P(),
            P(),
            P(None, None, "expert"),
            P(None, None, "expert"),
            P(None, "expert", None),
            P(),
            P("expert", None, None, "seq"),
            P("expert", "seq", None),
        ),
        out_specs=P("section", ("seq", "expert"), None),
        check_vma=False,
    )
```

profile of v0, /device:TPU:0, one launch (start us, length us, event | category | flops | bytes accessed | tf_op | source)
XLA Modules:
  0.0 696.3 jit_solution(16072841294543308900)
XLA Ops:
  6.5 7.7 %copy.140 = bf16[2048,4,256]{0,2,1:T(8,128)(2,1)} copy(bf16[2048,4,256]{2,1,0:T(4,128)(2,1)} %param.26) | data formatting | bytes 8388608 | tf_op jit(solution)/shard_map/while | solution.py:244
  14.3 4.8 copy.142
  19.2 660.6 %while.14 = (s32[]{:T(128)}, bf16[16,2048]{1,0:T(8,128)(2,1)S(1)}, bf16[3,16,2048]{2,1,0:T(8,128)(2,1)}, pred[]{:T(512)}, s32[3]{0:T(128)S(1)}, /*index=5*/bf16[...) while((s32[]{:T(128)}, bf16[16,2048]{1,0:T(8,128)(2,1)S(1)}, ...), condition=%wide.region_19.20_spmd, body=%wide.region_0.19_spmd.sunk | while | flops 6617626624 | bytes 126714792 | solution.py:244
  20.5 13.7 %all-gather.5 = bf16[1,128,2048]{2,1,0:T(8,128)(2,1)S(1)} all-gather(bf16[1,16,2048]{2,1,0:T(8,128)(2,1)S(1)} %constant_dynamic-slice_fusion.10), channel_id=2, replica_groups=mesh['section'=2,'seq'=8,'expert'=8] {'expert'}, dimensions={1}, use_global_device_ids=true | all-gather | bytes 589824 | tf_op jit(solution)/shard_map/while/body/eval_jaxpr/all_gather | solution.py:66
  34.5 2.4 fusion.208
  41.6 8.9 %all-to-all-start = ((bf16[64,8,2048]{2,1,0:T(8,128)(2,1)}), bf16[64,8,2048]{2,1,0:T(8,128)(2,1)}, u32[]{:S(2)}, u32[]{:S(2)}) async-start(bf16[64,8,2048]{2,1,0:T(8,128)(2,1)} %bitcast.287), calls=%async_computation | async-start | bytes 4194304 | tf_op jit(solution)/shard_map/while/body/eval_jaxpr/all_to_all | solution.py:173
  54.5 3.8 fusion.202
  60.6 2.4 gather_fusion.3
  65.5 37.0 %all-gather.11.cloned.1.call-done = bf16[1024,2,256]{0,2,1:T(8,128)(2,1)} async-done(((bf16[128,2,256]{0,2,1:T(8,128)(2,1)}), bf16[1024,2,256]{0,2,1:T(8,128)(2,1)}) %all-gather.11.cloned.1.call-update) | async-done | bytes 1048592 | tf_op jit(solution)/shard_map/while/body/eval_jaxpr/all_gather | solution.py:120
  102.5 2.1 fusion.209
  106.5 6.0 fusion.195
  112.6 3.4 fusion.196
  116.0 10.0 %all-to-all-start.1 = ((bf16[64,8,2048]{2,1,0:T(8,128)(2,1)}), bf16[64,8,2048]{2,1,0:T(8,128)(2,1)S(1)}, u32[]{:S(2)}, u32[]{:S(2)}) async-start(bf16[64,8,2048]{2,1,0:T(8,128)(2,1)} %fusion.196), calls=%async_computation.1 | async-start | bytes 4194304 | tf_op jit(solution)/shard_map/while/body/eval_jaxpr/all_to_all | solution.py:178
  126.0 60.6 %all-gather.9.cloned.1.call-done = bf16[1,2048,2,256]{1,3,2,0:T(8,128)(2,1)} async-done(((bf16[1,256,2,256]{1,3,2,0:T(8,128)(2,1)}), bf16[1,2048,2,256]{1,3,2,0:T(8,128)(2,1)}) %all-gather.9.cloned.1.call-update) | async-done | bytes 2097168 | tf_op jit(solution)/shard_map/while/body/eval_jaxpr/all_gather | solution.py:116
  195.3 3.7 fusion.216
  200.4 32.2 %reduce-scatter.2.cloned.1.call-done = bf16[16,2048]{1,0:T(8,128)(2,1)} async-done(((bf16[128,2048]{1,0:T(8,128)(2,1)}), bf16[16,2048]{1,0:T(8,128)(2,1)}) %reduce-scatter.2.cloned.1.call-update) | async-done | bytes 65552 | tf_op jit(solution)/shard_map/while/body/eval_jaxpr/reduce_scatter | solution.py:136
  234.1 5.1 collective-permute-start
  242.4 13.1 %all-gather.5 = bf16[1,128,2048]{2,1,0:T(8,128)(2,1)S(1)} all-gather(bf16[1,16,2048]{2,1,0:T(8,128)(2,1)S(1)} %constant_dynamic-slice_fusion.10), channel_id=2, replica_groups=mesh['section'=2,'seq'=8,'expert'=8] {'expert'}, dimensions={1}, use_global_device_ids=true | all-gather | bytes 589824 | tf_op jit(solution)/shard_map/while/body/eval_jaxpr/all_gather | solution.py:66
  255.7 2.4 fusion.208
  262.9 6.4 all-to-all-start
  273.3 3.7 fusion.202
  279.4 2.4 gather_fusion.3
  284.3 38.8 %all-gather.11.cloned.1.call-done = bf16[1024,2,256]{0,2,1:T(8,128)(2,1)} async-done(((bf16[128,2,256]{0,2,1:T(8,128)(2,1)}), bf16[1024,2,256]{0,2,1:T(8,128)(2,1)}) %all-gather.11.cloned.1.call-update) | async-done | bytes 1048592 | tf_op jit(solution)/shard_map/while/body/eval_jaxpr/all_gather | solution.py:120
  323.1 2.1 fusion.209
  325.2 2.0 fusion.210
  327.2 6.0 fusion.195
  333.3 3.4 fusion.196
  336.6 10.1 %all-to-all-start.1 = ((bf16[64,8,2048]{2,1,0:T(8,128)(2,1)}), bf16[64,8,2048]{2,1,0:T(8,128)(2,1)S(1)}, u32[]{:S(2)}, u32[]{:S(2)}) async-start(bf16[64,8,2048]{2,1,0:T(8,128)(2,1)} %fusion.196), calls=%async_computation.1 | async-start | bytes 4194304 | tf_op jit(solution)/shard_map/while/body/eval_jaxpr/all_to_all | solution.py:178
  346.8 62.6 %all-gather.9.cloned.1.call-done = bf16[1,2048,2,256]{1,3,2,0:T(8,128)(2,1)} async-done(((bf16[1,256,2,256]{1,3,2,0:T(8,128)(2,1)}), bf16[1,2048,2,256]{1,3,2,0:T(8,128)(2,1)}) %all-gather.9.cloned.1.call-update) | async-done | bytes 2097168 | tf_op jit(solution)/shard_map/while/body/eval_jaxpr/all_gather | solution.py:116
  418.1 3.7 fusion.216
  423.3 27.6 %reduce-scatter.2.cloned.1.call-done = bf16[16,2048]{1,0:T(8,128)(2,1)} async-done(((bf16[128,2048]{1,0:T(8,128)(2,1)}), bf16[16,2048]{1,0:T(8,128)(2,1)}) %reduce-scatter.2.cloned.1.call-update) | async-done | bytes 65552 | tf_op jit(solution)/shard_map/while/body/eval_jaxpr/reduce_scatter | solution.py:136
  452.5 4.9 collective-permute-start
  460.6 13.1 %all-gather.5 = bf16[1,128,2048]{2,1,0:T(8,128)(2,1)S(1)} all-gather(bf16[1,16,2048]{2,1,0:T(8,128)(2,1)S(1)} %constant_dynamic-slice_fusion.10), channel_id=2, replica_groups=mesh['section'=2,'seq'=8,'expert'=8] {'expert'}, dimensions={1}, use_global_device_ids=true | all-gather | bytes 589824 | tf_op jit(solution)/shard_map/while/body/eval_jaxpr/all_gather | solution.py:66
  473.9 2.4 fusion.208
  481.1 6.6 all-to-all-start
  491.7 3.7 fusion.202
  497.7 2.4 gather_fusion.3
  502.6 39.1 %all-gather.11.cloned.1.call-done = bf16[1024,2,256]{0,2,1:T(8,128)(2,1)} async-done(((bf16[128,2,256]{0,2,1:T(8,128)(2,1)}), bf16[1024,2,256]{0,2,1:T(8,128)(2,1)}) %all-gather.11.cloned.1.call-update) | async-done | bytes 1048592 | tf_op jit(solution)/shard_map/while/body/eval_jaxpr/all_gather | solution.py:120
  541.8 2.1 fusion.209
  543.9 2.0 fusion.210
  545.9 6.0 fusion.195
  551.9 3.4 fusion.196
  555.3 9.8 %all-to-all-start.1 = ((bf16[64,8,2048]{2,1,0:T(8,128)(2,1)}), bf16[64,8,2048]{2,1,0:T(8,128)(2,1)S(1)}, u32[]{:S(2)}, u32[]{:S(2)}) async-start(bf16[64,8,2048]{2,1,0:T(8,128)(2,1)} %fusion.196), calls=%async_computation.1 | async-start | bytes 4194304 | tf_op jit(solution)/shard_map/while/body/eval_jaxpr/all_to_all | solution.py:178
  565.2 64.6 %all-gather.9.cloned.1.call-done = bf16[1,2048,2,256]{1,3,2,0:T(8,128)(2,1)} async-done(((bf16[1,256,2,256]{1,3,2,0:T(8,128)(2,1)}), bf16[1,2048,2,256]{1,3,2,0:T(8,128)(2,1)}) %all-gather.9.cloned.1.call-update) | async-done | bytes 2097168 | tf_op jit(solution)/shard_map/while/body/eval_jaxpr/all_gather | solution.py:116
  638.5 3.7 fusion.216
  643.6 27.7 %reduce-scatter.2.cloned.1.call-done = bf16[16,2048]{1,0:T(8,128)(2,1)} async-done(((bf16[128,2048]{1,0:T(8,128)(2,1)}), bf16[16,2048]{1,0:T(8,128)(2,1)}) %reduce-scatter.2.cloned.1.call-update) | async-done | bytes 65552 | tf_op jit(solution)/shard_map/while/body/eval_jaxpr/reduce_scatter | solution.py:136
  672.9 5.0 collective-permute-start
  681.9 6.4 collective-permute-done.1
  (339 shorter events, 87.0 us)
Async XLA Ops:
  6.5 7.7 %copy-start.3 = (bf16[2048,2,256]{2,1,0:T(2,128)(2,1)S(1)}, bf16[2048,2,256]{2,1,0:T(2,128)(2,1)}, u32[]{:S(2)}) copy-start(bf16[2048,2,256]{2,1,0:T(2,128)(2,1)} %param.27) | copy-start | bytes 6291460
  14.2 4.9 copy-start.2
  14.2 4.9 copy-start.4
  14.2 4.9 copy-start.5
  14.3 4.9 copy-start.6
  14.3 4.9 copy-start.7
  14.3 4.9 copy-start.8
  14.3 4.9 copy-start.9
  14.3 4.9 copy-start.11
  14.3 4.9 copy-start.12
  19.2 83.3 %all-gather.11.cloned.1.call-start = ((), (), s32[]{:S(2)}) async-start(), calls=%async_computation.4 | async-start | bytes 1179648 | tf_op jit(solution)/shard_map/while/body/eval_jaxpr/all_gather | solution.py:120
  41.6 64.9 %all-to-all-start = ((bf16[64,8,2048]{2,1,0:T(8,128)(2,1)}), bf16[64,8,2048]{2,1,0:T(8,128)(2,1)}, u32[]{:S(2)}, u32[]{:S(2)}) async-start(bf16[64,8,2048]{2,1,0:T(8,128)(2,1)} %bitcast.287), calls=%async_computation | async-start | bytes 4194304 | tf_op jit(solution)/shard_map/while/body/eval_jaxpr/all_to_all | solution.py:173
  50.5 136.1 %all-gather.9.cloned.1.call-start = ((), (), s32[]{:S(2)}) async-start(), calls=%async_computation.3 | async-start | bytes 2359296 | tf_op jit(solution)/shard_map/while/body/eval_jaxpr/all_gather | solution.py:116
  106.5 6.0 copy-start.10
  116.0 83.1 %all-to-all-start.1 = ((bf16[64,8,2048]{2,1,0:T(8,128)(2,1)}), bf16[64,8,2048]{2,1,0:T(8,128)(2,1)S(1)}, u32[]{:S(2)}, u32[]{:S(2)}) async-start(bf16[64,8,2048]{2,1,0:T(8,128)(2,1)} %fusion.196), calls=%async_computation.1 | async-start | bytes 4194304 | tf_op jit(solution)/shard_map/while/body/eval_jaxpr/all_to_all | solution.py:178
  125.9 106.7 %reduce-scatter.2.cloned.1.call-start = ((), (), s32[]{:S(2)}) async-start(), calls=%async_computation.5 | async-start | bytes 589824 | tf_op jit(solution)/shard_map/while/body/eval_jaxpr/reduce_scatter | solution.py:136
  188.3 1.6 copy-start
  192.1 1.4 copy-start.1
  234.1 6.9 collective-permute-start
  241.1 82.0 %all-gather.11.cloned.1.call-start = ((), (), s32[]{:S(2)}) async-start(), calls=%async_computation.4 | async-start | bytes 1179648 | tf_op jit(solution)/shard_map/while/body/eval_jaxpr/all_gather | solution.py:120
  262.9 64.3 %all-to-all-start = ((bf16[64,8,2048]{2,1,0:T(8,128)(2,1)}), bf16[64,8,2048]{2,1,0:T(8,128)(2,1)}, u32[]{:S(2)}, u32[]{:S(2)}) async-start(bf16[64,8,2048]{2,1,0:T(8,128)(2,1)} %bitcast.287), calls=%async_computation | async-start | bytes 4194304 | tf_op jit(solution)/shard_map/while/body/eval_jaxpr/all_to_all | solution.py:173
  269.3 140.1 %all-gather.9.cloned.1.call-start = ((), (), s32[]{:S(2)}) async-start(), calls=%async_computation.3 | async-start | bytes 2359296 | tf_op jit(solution)/shard_map/while/body/eval_jaxpr/all_gather | solution.py:116
  327.2 6.1 copy-start.10
  336.6 85.3 %all-to-all-start.1 = ((bf16[64,8,2048]{2,1,0:T(8,128)(2,1)}), bf16[64,8,2048]{2,1,0:T(8,128)(2,1)S(1)}, u32[]{:S(2)}, u32[]{:S(2)}) async-start(bf16[64,8,2048]{2,1,0:T(8,128)(2,1)} %fusion.196), calls=%async_computation.1 | async-start | bytes 4194304 | tf_op jit(solution)/shard_map/while/body/eval_jaxpr/all_to_all | solution.py:178
  346.7 104.2 %reduce-scatter.2.cloned.1.call-start = ((), (), s32[]{:S(2)}) async-start(), calls=%async_computation.5 | async-start | bytes 589824 | tf_op jit(solution)/shard_map/while/body/eval_jaxpr/reduce_scatter | solution.py:136
  411.1 1.6 copy-start
  415.0 1.4 copy-start.1
  452.5 6.8 collective-permute-start
  459.3 82.5 %all-gather.11.cloned.1.call-start = ((), (), s32[]{:S(2)}) async-start(), calls=%async_computation.4 | async-start | bytes 1179648 | tf_op jit(solution)/shard_map/while/body/eval_jaxpr/all_gather | solution.py:120
  481.1 64.8 %all-to-all-start = ((bf16[64,8,2048]{2,1,0:T(8,128)(2,1)}), bf16[64,8,2048]{2,1,0:T(8,128)(2,1)}, u32[]{:S(2)}, u32[]{:S(2)}) async-start(bf16[64,8,2048]{2,1,0:T(8,128)(2,1)} %bitcast.287), calls=%async_computation | async-start | bytes 4194304 | tf_op jit(solution)/shard_map/while/body/eval_jaxpr/all_to_all | solution.py:173
  487.7 142.1 %all-gather.9.cloned.1.call-start = ((), (), s32[]{:S(2)}) async-start(), calls=%async_computation.3 | async-start | bytes 2359296 | tf_op jit(solution)/shard_map/while/body/eval_jaxpr/all_gather | solution.py:116
  545.9 6.0 copy-start.10
  555.3 87.0 %all-to-all-start.1 = ((bf16[64,8,2048]{2,1,0:T(8,128)(2,1)}), bf16[64,8,2048]{2,1,0:T(8,128)(2,1)S(1)}, u32[]{:S(2)}, u32[]{:S(2)}) async-start(bf16[64,8,2048]{2,1,0:T(8,128)(2,1)} %fusion.196), calls=%async_computation.1 | async-start | bytes 4194304 | tf_op jit(solution)/shard_map/while/body/eval_jaxpr/all_to_all | solution.py:178
  565.1 106.2 %reduce-scatter.2.cloned.1.call-start = ((), (), s32[]{:S(2)}) async-start(), calls=%async_computation.5 | async-start | bytes 589824 | tf_op jit(solution)/shard_map/while/body/eval_jaxpr/reduce_scatter | solution.py:136
  631.5 1.6 copy-start
  635.3 1.4 copy-start.1
  672.9 6.9 collective-permute-start
  680.6 7.7 %collective-permute-start.1 = (bf16[1,16,2048]{2,1,0:T(8,128)(2,1)S(1)}, bf16[1,16,2048]{2,1,0:T(8,128)(2,1)S(1)}, u32[]{:S(2)}, u32[]{:S(2)}) collective-permute-start(bf16[1,16,2048]{2,1,0:T(8,128)(2,1)S(1)} %slice.118), channel_id=1, source_target_pairs={{64,0},{65,1},{66,2},{67,3},{68,4},{69,5},{70,6},{71,7},{72,8},{73... | collective-permute-start | bytes 196616 | tf_op jit(solution)/shard_map/ppermute | solution.py:15
Sparse Core Ops, SparseCore 0:
  38.3 64.0 all-gather.10
  104.0 82.4 all-gather.8
  199.1 33.4 reduce-scatter.1
  259.6 63.4 all-gather.10
  324.5 84.8 all-gather.8
  422.0 28.8 reduce-scatter.1
  477.8 63.9 all-gather.10
  543.3 86.3 all-gather.8
  642.3 28.9 reduce-scatter.1
where the time goes:
time: 698 us; the launch traced here: 696 us
  waiting for transfers between devices  402 us (58%)
  matrix products  78.5 us (11%)
  starting transfers between devices  68.3 us (10%)
  local copies, waits for them, and re-layouts  62.6 us (9%)
  blocking collectives  39.9 us (6%)
  other arithmetic  26 us (4%)
  between operations  13.2 us (2%)
    all_gather x3, waiting for transfers between devices, attention_block(): piece = lax.all_gather(cache_rows, 'seq', axis=0, tiled=True)  188 us
    all_gather x3, waiting for transfers between devices, attention_block(): piece = lax.all_gather(fresh, 'seq', axis=0, tiled=True)  115 us
    reduce_scatter x3, waiting for transfers between devices, attention_block(): lax.psum_scatter(jnp.dot(spread, out_flat, preferred_element_type=jnp.flo...  87.5 us
    all_gather x3, blocking collectives, attention_block(): gathered = lax.all_gather(own_rows, 'expert', axis=0, tiled=True)  39.9 us
    all_to_all x3, starting transfers between devices, expert_block(): lax.all_to_all(partial_value, ('seq', 'expert'), split_axis=0, concat_axi...  29.9 us
    all_to_all x3, starting transfers between devices, expert_block(): lax.all_to_all(copies, ('seq', 'expert'), split_axis=0, concat_axis=0, ti...  21.9 us
    dot_general x3, matrix products, expert_hidden(): jnp.dot(rows, single.reshape(single.shape[0], -1), preferred_element_type...  18.1 us
    ppermute x4, starting transfers between devices, passed_along(): lax.ppermute(value, axis, [(source, source + steps) for source in range(i...  16.2 us
  transfers between devices with their start and end apart: 19, of which 13 were waited for; matrix products, arithmetic and copies ran while one was open for 19% of the time, Pallas kernels for 0%

commit v1 on v0

--- a/solution.py
+++ b/solution.py
@@ -117,7 +117,9 @@
     key_segment = segment_of(jnp.arange(piece.shape[0], dtype=jnp.int32), cached)
     allowed = query_segment[:, None] == key_segment[None, :]
     carried = absorb(initial, piece, allowed)
-    piece = lax.all_gather(fresh, "seq", axis=0, tiled=True)
+    piece = jnp.concatenate(
+        lax.all_to_all(jnp.stack([fresh] * lax.axis_size("seq")), "seq", 0, 0), axis=0
+    )
     key_index = jnp.arange(piece.shape[0], dtype=jnp.int32)
     key_segment = segment_of(key_index, lengths)
     allowed = (query_segment[:, None] == key_segment[None, :]) & (

time: 698 us -> 510 us (0.73)
  waiting for transfers between devices: 402 us -> 198 us
  starting transfers between devices: 68.3 us -> 84.8 us
    all_gather x3, waiting for transfers between devices: 188 us -> 0.06 us  [attention_block(): piece = lax.all_gather(cache_rows, 'seq', axis=0, tiled=True)]
    all_gather x3 -> x0, waiting for transfers between devices: 115 us -> none  [attention_block(): piece = lax.all_gather(fresh, 'seq', axis=0, tiled=True)]
    all_to_all x3, waiting for transfers between devices: 0.01 us -> 67.5 us  [expert_block(): lax.all_to_all(copies, ('seq', 'expert'), split_axis=0, concat_axis=0, ti...]
    all_to_all x3, waiting for transfers between devices: 0.01 us -> 48.3 us  [expert_block(): lax.all_to_all(partial_value, ('seq', 'expert'), split_axis=0, concat_axi...]
    reduce_scatter x3, waiting for transfers between devices: 87.5 us -> 43.7 us  [attention_block(): lax.psum_scatter(jnp.dot(spread, out_flat, preferred_element_type=jnp.flo...]
    all_to_all x0 -> x3, waiting for transfers between devices: none -> 26 us  [attention_block(): lax.all_to_all(jnp.stack([fresh] * lax.axis_size('seq')), 'seq', 0, 0)]
    all_to_all x0 -> x3, starting transfers between devices: none -> 15.2 us  [attention_block(): lax.all_to_all(jnp.stack([fresh] * lax.axis_size('seq')), 'seq', 0, 0)]
  transfers between devices with their start and end apart: 19 -> 19, of which waited for: 13 -> 16; matrix products, arithmetic and copies ran while one was open for 19% -> 27% of each run, Pallas kernels for 0% -> 0%
where the time goes in v1:
time: 510 us; the launch traced here: 507 us
  waiting for transfers between devices  198 us (39%)
  starting transfers between devices  84.8 us (17%)
  matrix products  78.2 us (15%)
  local copies, waits for them, and re-layouts  63.5 us (12%)
  blocking collectives  39.9 us (8%)
  other arithmetic  24.1 us (5%)
  between operations  13.5 us (3%)
  loops' own time  5.28 us (1%)
    all_to_all x3, waiting for transfers between devices, expert_block(): lax.all_to_all(copies, ('seq', 'expert'), split_axis=0, concat_axis=0, ti...  67.5 us
    all_to_all x3, waiting for transfers between devices, expert_block(): lax.all_to_all(partial_value, ('seq', 'expert'), split_axis=0, concat_axi...  48.3 us
    reduce_scatter x3, waiting for transfers between devices, attention_block(): lax.psum_scatter(jnp.dot(spread, out_flat, preferred_element_type=jnp.flo...  43.7 us
    all_gather x3, blocking collectives, attention_block(): gathered = lax.all_gather(own_rows, 'expert', axis=0, tiled=True)  39.9 us
    all_to_all x3, starting transfers between devices, expert_block(): lax.all_to_all(partial_value, ('seq', 'expert'), split_axis=0, concat_axi...  29.7 us
    all_to_all x3, waiting for transfers between devices, attention_block(): lax.all_to_all(jnp.stack([fresh] * lax.axis_size('seq')), 'seq', 0, 0)  26 us
    all_to_all x3, starting transfers between devices, expert_block(): lax.all_to_all(copies, ('seq', 'expert'), split_axis=0, concat_axis=0, ti...  23 us
    dot_general x3, matrix products, expert_hidden(): jnp.dot(rows, single.reshape(single.shape[0], -1), preferred_element_type...  18.1 us
  transfers between devices with their start and end apart: 19, of which 16 were waited for; matrix products, arithmetic and copies ran while one was open for 27% of the time, Pallas kernels for 0%

profile of v1, /device:TPU:0, one launch (start us, length us, event | category | flops | bytes accessed | tf_op | source)
XLA Modules:
  0.0 507.0 jit_solution(8303923412617056251)
XLA Ops:
  6.5 7.7 %copy.145 = bf16[2048,4,256]{0,2,1:T(8,128)(2,1)} copy(bf16[2048,4,256]{2,1,0:T(4,128)(2,1)} %param.26) | data formatting | bytes 8388608 | tf_op jit(solution)/shard_map/while | solution.py:246
  14.3 4.8 copy.147
  19.2 471.0 %while.14 = (s32[]{:T(128)}, bf16[16,2048]{1,0:T(8,128)(2,1)S(1)}, bf16[3,16,2048]{2,1,0:T(8,128)(2,1)}, pred[]{:T(512)}, s32[3]{0:T(128)S(1)}, /*index=5*/bf16[...) while((s32[]{:T(128)}, bf16[16,2048]{1,0:T(8,128)(2,1)S(1)}, ...), condition=%wide.region_19.20_spmd, body=%wide.region_0.19_spmd.sunk | while | flops 6617626624 | bytes 129598360 | solution.py:246
  22.6 13.7 %all-gather.5 = bf16[1,128,2048]{2,1,0:T(8,128)(2,1)S(1)} all-gather(bf16[1,16,2048]{2,1,0:T(8,128)(2,1)S(1)} %constant_dynamic-slice_fusion.10), channel_id=2, replica_groups=mesh['section'=2,'seq'=8,'expert'=8] {'expert'}, dimensions={1}, use_global_device_ids=true | all-gather | bytes 589824 | tf_op jit(solution)/shard_map/while/body/eval_jaxpr/all_gather | solution.py:66
  36.5 2.4 fusion.211
  40.9 5.7 %all-to-all-start.2 = ((bf16[8,128,2,256]{1,3,2,0:T(8,128)(2,1)}), bf16[8,128,2,256]{1,3,2,0:T(8,128)(2,1)S(1)}, u32[]{:S(2)}, u32[]{:S(2)}) async-start(bf16[8,128,2,256]{1,3,2,0:T(8,128)(2,1)} %stack.13), calls=%async_computation.2 | async-start | bytes 2097152 | tf_op jit(solution)/shard_map/while/body/eval_jaxpr/all_to_all | solution.py:121
  50.1 2.4 gather_fusion.3
  52.9 3.7 fusion.205
  57.0 8.2 %all-to-all-done.2 = bf16[8,128,2,256]{1,3,2,0:T(8,128)(2,1)S(1)} async-done(((bf16[8,128,2,256]{1,3,2,0:T(8,128)(2,1)}), bf16[8,128,2,256]{1,3,2,0:T(8,128)(2,1)S(1)}, u32[]{:S(2)}, u32[]{:S(2)}) %all-to-all-start.2) | async-done | bytes 1048608 | tf_op jit(solution)/shard_map/while/body/eval_jaxpr/all_to_all | solution.py:121
  66.8 8.9 %all-to-all-start = ((bf16[64,8,2048]{2,1,0:T(8,128)(2,1)}), bf16[64,8,2048]{2,1,0:T(8,128)(2,1)}, u32[]{:S(2)}, u32[]{:S(2)}) async-start(bf16[64,8,2048]{2,1,0:T(8,128)(2,1)} %bitcast.296), calls=%async_computation | async-start | bytes 4194304 | tf_op jit(solution)/shard_map/while/body/eval_jaxpr/all_to_all | solution.py:175
  82.9 23.3 %all-to-all-done = bf16[64,8,2048]{2,1,0:T(8,128)(2,1)} async-done(((bf16[64,8,2048]{2,1,0:T(8,128)(2,1)}), bf16[64,8,2048]{2,1,0:T(8,128)(2,1)}, u32[]{:S(2)}, u32[]{:S(2)}) %all-to-all-start) | async-done | bytes 2097184 | tf_op jit(solution)/shard_map/while/body/eval_jaxpr/all_to_all | solution.py:175
  106.2 6.0 %fusion.198 = f32[512,2,704]{0,2,1:T(8,128)S(1)} fusion(bf16[1,2048,2,704]{1,3,2,0:T(8,128)(2,1)} %get-tuple-element.722, bf16[64,8,2048]{2,1,0:T(8,128)(2,1)} %all-to-all-done), kind=kOutput, calls=%fused_computation.4.clone.1 | convolution fusion | flops 2952790016 | bytes 10747904 | tf_op jit(solution)/shard_map/while/body/eval_jaxpr/dot_general | solution.py:149
  112.3 3.4 fusion.199
  115.6 6.1 %all-to-all-start.1 = ((bf16[64,8,2048]{2,1,0:T(8,128)(2,1)}), bf16[64,8,2048]{2,1,0:T(8,128)(2,1)S(1)}, u32[]{:S(2)}, u32[]{:S(2)}) async-start(bf16[64,8,2048]{2,1,0:T(8,128)(2,1)} %fusion.199), calls=%async_computation.1 | async-start | bytes 4194304 | tf_op jit(solution)/shard_map/while/body/eval_jaxpr/all_to_all | solution.py:180
  130.5 3.7 fusion.219
  134.3 16.1 %all-to-all-done.1 = bf16[64,8,2048]{2,1,0:T(8,128)(2,1)S(1)} async-done(((bf16[64,8,2048]{2,1,0:T(8,128)(2,1)}), bf16[64,8,2048]{2,1,0:T(8,128)(2,1)S(1)}, u32[]{:S(2)}, u32[]{:S(2)}) %all-to-all-start.1) | async-done | bytes 2097184 | tf_op jit(solution)/shard_map/while/body/eval_jaxpr/all_to_all | solution.py:180
  151.7 16.7 %reduce-scatter.2.cloned.1.call-done = bf16[16,2048]{1,0:T(8,128)(2,1)} async-done(((bf16[128,2048]{1,0:T(8,128)(2,1)}), bf16[16,2048]{1,0:T(8,128)(2,1)}) %reduce-scatter.2.cloned.1.call-update) | async-done | bytes 65552 | tf_op jit(solution)/shard_map/while/body/eval_jaxpr/reduce_scatter | solution.py:138
  170.0 5.2 %collective-permute-start = (bf16[16,2048]{1,0:T(8,128)(2,1)S(1)}, bf16[16,2048]{1,0:T(8,128)(2,1)S(1)}, u32[]{:S(2)}, u32[]{:S(2)}) collective-permute-start(bf16[16,2048]{1,0:T(8,128)(2,1)S(1)} %get-tuple-element.644), channel_id=1, source_target_pairs={{0,64},{1,65},{2,66},{3,67},{4,68},{5,69},{6,70},{7,71},{8,72},{9,... | collective-permute-start | bytes 196616 | tf_op jit(solution)/shard_map/while/body/eval_jaxpr/ppermute | solution.py:15
  180.4 13.1 %all-gather.5 = bf16[1,128,2048]{2,1,0:T(8,128)(2,1)S(1)} all-gather(bf16[1,16,2048]{2,1,0:T(8,128)(2,1)S(1)} %constant_dynamic-slice_fusion.10), channel_id=2, replica_groups=mesh['section'=2,'seq'=8,'expert'=8] {'expert'}, dimensions={1}, use_global_device_ids=true | all-gather | bytes 589824 | tf_op jit(solution)/shard_map/while/body/eval_jaxpr/all_gather | solution.py:66
  193.7 2.4 fusion.211
  198.1 4.8 all-to-all-start.2
  206.4 2.4 gather_fusion.3
  209.2 3.7 fusion.205
  213.3 8.9 %all-to-all-done.2 = bf16[8,128,2,256]{1,3,2,0:T(8,128)(2,1)S(1)} async-done(((bf16[8,128,2,256]{1,3,2,0:T(8,128)(2,1)}), bf16[8,128,2,256]{1,3,2,0:T(8,128)(2,1)S(1)}, u32[]{:S(2)}, u32[]{:S(2)}) %all-to-all-start.2) | async-done | bytes 1048608 | tf_op jit(solution)/shard_map/while/body/eval_jaxpr/all_to_all | solution.py:121
  223.8 7.1 %all-to-all-start = ((bf16[64,8,2048]{2,1,0:T(8,128)(2,1)}), bf16[64,8,2048]{2,1,0:T(8,128)(2,1)}, u32[]{:S(2)}, u32[]{:S(2)}) async-start(bf16[64,8,2048]{2,1,0:T(8,128)(2,1)} %bitcast.296), calls=%async_computation | async-start | bytes 4194304 | tf_op jit(solution)/shard_map/while/body/eval_jaxpr/all_to_all | solution.py:175
  238.1 22.1 %all-to-all-done = bf16[64,8,2048]{2,1,0:T(8,128)(2,1)} async-done(((bf16[64,8,2048]{2,1,0:T(8,128)(2,1)}), bf16[64,8,2048]{2,1,0:T(8,128)(2,1)}, u32[]{:S(2)}, u32[]{:S(2)}) %all-to-all-start) | async-done | bytes 2097184 | tf_op jit(solution)/shard_map/while/body/eval_jaxpr/all_to_all | solution.py:175
  260.2 6.0 %fusion.198 = f32[512,2,704]{0,2,1:T(8,128)S(1)} fusion(bf16[1,2048,2,704]{1,3,2,0:T(8,128)(2,1)} %get-tuple-element.722, bf16[64,8,2048]{2,1,0:T(8,128)(2,1)} %all-to-all-done), kind=kOutput, calls=%fused_computation.4.clone.1 | convolution fusion | flops 2952790016 | bytes 10747904 | tf_op jit(solution)/shard_map/while/body/eval_jaxpr/dot_general | solution.py:149
  266.2 3.4 fusion.199
  269.6 11.8 %all-to-all-start.1 = ((bf16[64,8,2048]{2,1,0:T(8,128)(2,1)}), bf16[64,8,2048]{2,1,0:T(8,128)(2,1)S(1)}, u32[]{:S(2)}, u32[]{:S(2)}) async-start(bf16[64,8,2048]{2,1,0:T(8,128)(2,1)} %fusion.199), calls=%async_computation.1 | async-start | bytes 4194304 | tf_op jit(solution)/shard_map/while/body/eval_jaxpr/all_to_all | solution.py:180
  290.3 3.7 fusion.219
  294.0 16.1 %all-to-all-done.1 = bf16[64,8,2048]{2,1,0:T(8,128)(2,1)S(1)} async-done(((bf16[64,8,2048]{2,1,0:T(8,128)(2,1)}), bf16[64,8,2048]{2,1,0:T(8,128)(2,1)S(1)}, u32[]{:S(2)}, u32[]{:S(2)}) %all-to-all-start.1) | async-done | bytes 2097184 | tf_op jit(solution)/shard_map/while/body/eval_jaxpr/all_to_all | solution.py:180
  311.5 13.5 %reduce-scatter.2.cloned.1.call-done = bf16[16,2048]{1,0:T(8,128)(2,1)} async-done(((bf16[128,2048]{1,0:T(8,128)(2,1)}), bf16[16,2048]{1,0:T(8,128)(2,1)}) %reduce-scatter.2.cloned.1.call-update) | async-done | bytes 65552 | tf_op jit(solution)/shard_map/while/body/eval_jaxpr/reduce_scatter | solution.py:138
  326.6 5.1 %collective-permute-start = (bf16[16,2048]{1,0:T(8,128)(2,1)S(1)}, bf16[16,2048]{1,0:T(8,128)(2,1)S(1)}, u32[]{:S(2)}, u32[]{:S(2)}) collective-permute-start(bf16[16,2048]{1,0:T(8,128)(2,1)S(1)} %get-tuple-element.644), channel_id=1, source_target_pairs={{0,64},{1,65},{2,66},{3,67},{4,68},{5,69},{6,70},{7,71},{8,72},{9,... | collective-permute-start | bytes 196616 | tf_op jit(solution)/shard_map/while/body/eval_jaxpr/ppermute | solution.py:15
  337.0 13.1 %all-gather.5 = bf16[1,128,2048]{2,1,0:T(8,128)(2,1)S(1)} all-gather(bf16[1,16,2048]{2,1,0:T(8,128)(2,1)S(1)} %constant_dynamic-slice_fusion.10), channel_id=2, replica_groups=mesh['section'=2,'seq'=8,'expert'=8] {'expert'}, dimensions={1}, use_global_device_ids=true | all-gather | bytes 589824 | tf_op jit(solution)/shard_map/while/body/eval_jaxpr/all_gather | solution.py:66
  354.6 4.8 all-to-all-start.2
  363.0 2.4 gather_fusion.3
  365.7 3.7 fusion.205
  369.8 8.9 %all-to-all-done.2 = bf16[8,128,2,256]{1,3,2,0:T(8,128)(2,1)S(1)} async-done(((bf16[8,128,2,256]{1,3,2,0:T(8,128)(2,1)}), bf16[8,128,2,256]{1,3,2,0:T(8,128)(2,1)S(1)}, u32[]{:S(2)}, u32[]{:S(2)}) %all-to-all-start.2) | async-done | bytes 1048608 | tf_op jit(solution)/shard_map/while/body/eval_jaxpr/all_to_all | solution.py:121
  380.3 7.1 %all-to-all-start = ((bf16[64,8,2048]{2,1,0:T(8,128)(2,1)}), bf16[64,8,2048]{2,1,0:T(8,128)(2,1)}, u32[]{:S(2)}, u32[]{:S(2)}) async-start(bf16[64,8,2048]{2,1,0:T(8,128)(2,1)} %bitcast.296), calls=%async_computation | async-start | bytes 4194304 | tf_op jit(solution)/shard_map/while/body/eval_jaxpr/all_to_all | solution.py:175
  394.7 22.1 %all-to-all-done = bf16[64,8,2048]{2,1,0:T(8,128)(2,1)} async-done(((bf16[64,8,2048]{2,1,0:T(8,128)(2,1)}), bf16[64,8,2048]{2,1,0:T(8,128)(2,1)}, u32[]{:S(2)}, u32[]{:S(2)}) %all-to-all-start) | async-done | bytes 2097184 | tf_op jit(solution)/shard_map/while/body/eval_jaxpr/all_to_all | solution.py:175
  416.8 6.0 %fusion.198 = f32[512,2,704]{0,2,1:T(8,128)S(1)} fusion(bf16[1,2048,2,704]{1,3,2,0:T(8,128)(2,1)} %get-tuple-element.722, bf16[64,8,2048]{2,1,0:T(8,128)(2,1)} %all-to-all-done), kind=kOutput, calls=%fused_computation.4.clone.1 | convolution fusion | flops 2952790016 | bytes 10747904 | tf_op jit(solution)/shard_map/while/body/eval_jaxpr/dot_general | solution.py:149
  422.8 3.4 fusion.199
  426.2 11.8 %all-to-all-start.1 = ((bf16[64,8,2048]{2,1,0:T(8,128)(2,1)}), bf16[64,8,2048]{2,1,0:T(8,128)(2,1)S(1)}, u32[]{:S(2)}, u32[]{:S(2)}) async-start(bf16[64,8,2048]{2,1,0:T(8,128)(2,1)} %fusion.199), calls=%async_computation.1 | async-start | bytes 4194304 | tf_op jit(solution)/shard_map/while/body/eval_jaxpr/all_to_all | solution.py:180
  446.8 3.7 fusion.219
  450.6 16.1 %all-to-all-done.1 = bf16[64,8,2048]{2,1,0:T(8,128)(2,1)S(1)} async-done(((bf16[64,8,2048]{2,1,0:T(8,128)(2,1)}), bf16[64,8,2048]{2,1,0:T(8,128)(2,1)S(1)}, u32[]{:S(2)}, u32[]{:S(2)}) %all-to-all-start.1) | async-done | bytes 2097184 | tf_op jit(solution)/shard_map/while/body/eval_jaxpr/all_to_all | solution.py:180
  468.0 13.5 %reduce-scatter.2.cloned.1.call-done = bf16[16,2048]{1,0:T(8,128)(2,1)} async-done(((bf16[128,2048]{1,0:T(8,128)(2,1)}), bf16[16,2048]{1,0:T(8,128)(2,1)}) %reduce-scatter.2.cloned.1.call-update) | async-done | bytes 65552 | tf_op jit(solution)/shard_map/while/body/eval_jaxpr/reduce_scatter | solution.py:138
  483.1 5.2 %collective-permute-start = (bf16[16,2048]{1,0:T(8,128)(2,1)S(1)}, bf16[16,2048]{1,0:T(8,128)(2,1)S(1)}, u32[]{:S(2)}, u32[]{:S(2)}) collective-permute-start(bf16[16,2048]{1,0:T(8,128)(2,1)S(1)} %get-tuple-element.644), channel_id=1, source_target_pairs={{0,64},{1,65},{2,66},{3,67},{4,68},{5,69},{6,70},{7,71},{8,72},{9,... | collective-permute-start | bytes 196616 | tf_op jit(solution)/shard_map/while/body/eval_jaxpr/ppermute | solution.py:15
  492.3 6.4 %collective-permute-done.1 = bf16[1,16,2048]{2,1,0:T(8,128)(2,1)S(1)} collective-permute-done((bf16[1,16,2048]{2,1,0:T(8,128)(2,1)S(1)}, bf16[1,16,2048]{2,1,0:T(8,128)(2,1)S(1)}, u32[]{:S(2)}, u32[]{:S(2)}) %collective-permute-start.1) | collective-permute-done | bytes 65568 | tf_op jit(solution)/shard_map/ppermute | solution.py:15
  (342 shorter events, 98.2 us)
Async XLA Ops:
  6.5 7.7 %copy-start.3 = (bf16[2048,2,256]{2,1,0:T(2,128)(2,1)S(1)}, bf16[2048,2,256]{2,1,0:T(2,128)(2,1)}, u32[]{:S(2)}) copy-start(bf16[2048,2,256]{2,1,0:T(2,128)(2,1)} %param.27) | copy-start | bytes 6291460
  14.2 4.9 copy-start.2
  14.2 4.9 copy-start.4
  14.2 4.9 copy-start.5
  14.3 4.9 copy-start.6
  14.3 4.9 copy-start.7
  14.3 4.9 copy-start.8
  14.3 4.9 copy-start.9
  14.3 4.9 copy-start.11
  14.3 4.9 copy-start.12
  19.2 102.6 %all-gather.8.cloned.1.call-start = ((), (), s32[]{:S(2)}) async-start(), calls=%async_computation.4 | async-start | bytes 2359296 | tf_op jit(solution)/shard_map/while/body/eval_jaxpr/all_gather | solution.py:116
  40.9 24.2 %all-to-all-start.2 = ((bf16[8,128,2,256]{1,3,2,0:T(8,128)(2,1)}), bf16[8,128,2,256]{1,3,2,0:T(8,128)(2,1)S(1)}, u32[]{:S(2)}, u32[]{:S(2)}) async-start(bf16[8,128,2,256]{1,3,2,0:T(8,128)(2,1)} %stack.13), calls=%async_computation.2 | async-start | bytes 2097152 | tf_op jit(solution)/shard_map/while/body/eval_jaxpr/all_to_all | solution.py:121
  66.8 39.4 %all-to-all-start = ((bf16[64,8,2048]{2,1,0:T(8,128)(2,1)}), bf16[64,8,2048]{2,1,0:T(8,128)(2,1)}, u32[]{:S(2)}, u32[]{:S(2)}) async-start(bf16[64,8,2048]{2,1,0:T(8,128)(2,1)} %bitcast.296), calls=%async_computation | async-start | bytes 4194304 | tf_op jit(solution)/shard_map/while/body/eval_jaxpr/all_to_all | solution.py:175
  106.2 6.0 %copy-start.10 = (bf16[1,704,2048]{2,1,0:T(8,128)(2,1)S(1)}, bf16[1,704,2048]{2,1,0:T(8,128)(2,1)}, u32[]{:S(2)}) copy-start(bf16[1,704,2048]{2,1,0:T(8,128)(2,1)} %get-tuple-element.723) | copy-start | bytes 8650756 | tf_op jit(solution)/shard_map/while
  115.6 34.8 %all-to-all-start.1 = ((bf16[64,8,2048]{2,1,0:T(8,128)(2,1)}), bf16[64,8,2048]{2,1,0:T(8,128)(2,1)S(1)}, u32[]{:S(2)}, u32[]{:S(2)}) async-start(bf16[64,8,2048]{2,1,0:T(8,128)(2,1)} %fusion.199), calls=%async_computation.1 | async-start | bytes 4194304 | tf_op jit(solution)/shard_map/while/body/eval_jaxpr/all_to_all | solution.py:180
  121.7 46.7 %reduce-scatter.2.cloned.1.call-start = ((), (), s32[]{:S(2)}) async-start(), calls=%async_computation.5 | async-start | bytes 589824 | tf_op jit(solution)/shard_map/while/body/eval_jaxpr/reduce_scatter | solution.py:138
  123.5 1.6 copy-start
  127.3 1.4 copy-start.1
  170.0 7.1 %collective-permute-start = (bf16[16,2048]{1,0:T(8,128)(2,1)S(1)}, bf16[16,2048]{1,0:T(8,128)(2,1)S(1)}, u32[]{:S(2)}, u32[]{:S(2)}) collective-permute-start(bf16[16,2048]{1,0:T(8,128)(2,1)S(1)} %get-tuple-element.644), channel_id=1, source_target_pairs={{0,64},{1,65},{2,66},{3,67},{4,68},{5,69},{6,70},{7,71},{8,72},{9,... | collective-permute-start | bytes 196616 | tf_op jit(solution)/shard_map/while/body/eval_jaxpr/ppermute | solution.py:15
  177.1 104.5 %all-gather.8.cloned.1.call-start = ((), (), s32[]{:S(2)}) async-start(), calls=%async_computation.4 | async-start | bytes 2359296 | tf_op jit(solution)/shard_map/while/body/eval_jaxpr/all_gather | solution.py:116
  198.1 24.1 %all-to-all-start.2 = ((bf16[8,128,2,256]{1,3,2,0:T(8,128)(2,1)}), bf16[8,128,2,256]{1,3,2,0:T(8,128)(2,1)S(1)}, u32[]{:S(2)}, u32[]{:S(2)}) async-start(bf16[8,128,2,256]{1,3,2,0:T(8,128)(2,1)} %stack.13), calls=%async_computation.2 | async-start | bytes 2097152 | tf_op jit(solution)/shard_map/while/body/eval_jaxpr/all_to_all | solution.py:121
  223.8 36.4 %all-to-all-start = ((bf16[64,8,2048]{2,1,0:T(8,128)(2,1)}), bf16[64,8,2048]{2,1,0:T(8,128)(2,1)}, u32[]{:S(2)}, u32[]{:S(2)}) async-start(bf16[64,8,2048]{2,1,0:T(8,128)(2,1)} %bitcast.296), calls=%async_computation | async-start | bytes 4194304 | tf_op jit(solution)/shard_map/while/body/eval_jaxpr/all_to_all | solution.py:175
  260.2 6.0 %copy-start.10 = (bf16[1,704,2048]{2,1,0:T(8,128)(2,1)S(1)}, bf16[1,704,2048]{2,1,0:T(8,128)(2,1)}, u32[]{:S(2)}) copy-start(bf16[1,704,2048]{2,1,0:T(8,128)(2,1)} %get-tuple-element.723) | copy-start | bytes 8650756 | tf_op jit(solution)/shard_map/while
  269.6 40.5 %all-to-all-start.1 = ((bf16[64,8,2048]{2,1,0:T(8,128)(2,1)}), bf16[64,8,2048]{2,1,0:T(8,128)(2,1)S(1)}, u32[]{:S(2)}, u32[]{:S(2)}) async-start(bf16[64,8,2048]{2,1,0:T(8,128)(2,1)} %fusion.199), calls=%async_computation.1 | async-start | bytes 4194304 | tf_op jit(solution)/shard_map/while/body/eval_jaxpr/all_to_all | solution.py:180
  281.5 43.5 %reduce-scatter.2.cloned.1.call-start = ((), (), s32[]{:S(2)}) async-start(), calls=%async_computation.5 | async-start | bytes 589824 | tf_op jit(solution)/shard_map/while/body/eval_jaxpr/reduce_scatter | solution.py:138
  283.3 1.6 copy-start
  287.1 1.4 copy-start.1
  326.6 7.0 %collective-permute-start = (bf16[16,2048]{1,0:T(8,128)(2,1)S(1)}, bf16[16,2048]{1,0:T(8,128)(2,1)S(1)}, u32[]{:S(2)}, u32[]{:S(2)}) collective-permute-start(bf16[16,2048]{1,0:T(8,128)(2,1)S(1)} %get-tuple-element.644), channel_id=1, source_target_pairs={{0,64},{1,65},{2,66},{3,67},{4,68},{5,69},{6,70},{7,71},{8,72},{9,... | collective-permute-start | bytes 196616 | tf_op jit(solution)/shard_map/while/body/eval_jaxpr/ppermute | solution.py:15
  333.6 104.5 %all-gather.8.cloned.1.call-start = ((), (), s32[]{:S(2)}) async-start(), calls=%async_computation.4 | async-start | bytes 2359296 | tf_op jit(solution)/shard_map/while/body/eval_jaxpr/all_gather | solution.py:116
  354.6 24.1 %all-to-all-start.2 = ((bf16[8,128,2,256]{1,3,2,0:T(8,128)(2,1)}), bf16[8,128,2,256]{1,3,2,0:T(8,128)(2,1)S(1)}, u32[]{:S(2)}, u32[]{:S(2)}) async-start(bf16[8,128,2,256]{1,3,2,0:T(8,128)(2,1)} %stack.13), calls=%async_computation.2 | async-start | bytes 2097152 | tf_op jit(solution)/shard_map/while/body/eval_jaxpr/all_to_all | solution.py:121
  380.3 36.4 %all-to-all-start = ((bf16[64,8,2048]{2,1,0:T(8,128)(2,1)}), bf16[64,8,2048]{2,1,0:T(8,128)(2,1)}, u32[]{:S(2)}, u32[]{:S(2)}) async-start(bf16[64,8,2048]{2,1,0:T(8,128)(2,1)} %bitcast.296), calls=%async_computation | async-start | bytes 4194304 | tf_op jit(solution)/shard_map/while/body/eval_jaxpr/all_to_all | solution.py:175
  416.8 6.0 %copy-start.10 = (bf16[1,704,2048]{2,1,0:T(8,128)(2,1)S(1)}, bf16[1,704,2048]{2,1,0:T(8,128)(2,1)}, u32[]{:S(2)}) copy-start(bf16[1,704,2048]{2,1,0:T(8,128)(2,1)} %get-tuple-element.723) | copy-start | bytes 8650756 | tf_op jit(solution)/shard_map/while
  426.2 40.5 %all-to-all-start.1 = ((bf16[64,8,2048]{2,1,0:T(8,128)(2,1)}), bf16[64,8,2048]{2,1,0:T(8,128)(2,1)S(1)}, u32[]{:S(2)}, u32[]{:S(2)}) async-start(bf16[64,8,2048]{2,1,0:T(8,128)(2,1)} %fusion.199), calls=%async_computation.1 | async-start | bytes 4194304 | tf_op jit(solution)/shard_map/while/body/eval_jaxpr/all_to_all | solution.py:180
  438.0 43.5 %reduce-scatter.2.cloned.1.call-start = ((), (), s32[]{:S(2)}) async-start(), calls=%async_computation.5 | async-start | bytes 589824 | tf_op jit(solution)/shard_map/while/body/eval_jaxpr/reduce_scatter | solution.py:138
  439.8 1.6 copy-start
  443.6 1.4 copy-start.1
  483.1 7.1 %collective-permute-start = (bf16[16,2048]{1,0:T(8,128)(2,1)S(1)}, bf16[16,2048]{1,0:T(8,128)(2,1)S(1)}, u32[]{:S(2)}, u32[]{:S(2)}) collective-permute-start(bf16[16,2048]{1,0:T(8,128)(2,1)S(1)} %get-tuple-element.644), channel_id=1, source_target_pairs={{0,64},{1,65},{2,66},{3,67},{4,68},{5,69},{6,70},{7,71},{8,72},{9,... | collective-permute-start | bytes 196616 | tf_op jit(solution)/shard_map/while/body/eval_jaxpr/ppermute | solution.py:15
  491.1 7.7 %collective-permute-start.1 = (bf16[1,16,2048]{2,1,0:T(8,128)(2,1)S(1)}, bf16[1,16,2048]{2,1,0:T(8,128)(2,1)S(1)}, u32[]{:S(2)}, u32[]{:S(2)}) collective-permute-start(bf16[1,16,2048]{2,1,0:T(8,128)(2,1)S(1)} %slice.118), channel_id=1, source_target_pairs={{64,0},{65,1},{66,2},{67,3},{68,4},{69,5},{70,6},{71,7},{72,8},{73... | collective-permute-start | bytes 196616 | tf_op jit(solution)/shard_map/ppermute | solution.py:15
Sparse Core Ops, SparseCore 0:
  22.7 94.1 all-gather.7
  134.4 34.0 reduce-scatter.1
  180.5 90.2 all-gather.7
  294.1 30.8 reduce-scatter.1
  337.0 90.3 all-gather.7
  450.6 30.8 reduce-scatter.1
